TPU v7x, 32 devices: a whole 2x2x4 slice. The times are simulated.
32 devices in a mesh: grp: 4 (over z), dom: 8 (over y, x, core).
Axes of the slice: x: 2, y: 2, z: 4, core: 2. Of those that a mesh axis runs over, the one named last changes fastest.
Arguments:
- local_inverse: bfloat16 [160, 640, 640], P(('grp', 'dom')), may hold values from -0.25 to 0.25
- local_trace: bfloat16 [160, 640, 480], P(('grp', 'dom')), may hold values from -0.25 to 0.25
- trace_local: bfloat16 [160, 480, 640], P(('grp', 'dom')), may hold values from -0.25 to 0.25
- trace_trace: bfloat16 [160, 480, 480], P(('grp', 'dom')), may hold values from -0.25 to 0.25
- local_rhs: bfloat16 [160, 640], P(('grp', 'dom')), may hold values from -6 to 6
- trace_rhs: bfloat16 [160, 480], P(('grp', 'dom')), may hold values from -6 to 6
- trace_state: bfloat16 [480, 80], P(('grp', 'dom')), may hold values from -6 to 6
- side_owner: int32 [160, 6], P(('grp', 'dom')), may hold values from 0 to 31, as said below
- side_slot: int32 [160, 6], P(('grp', 'dom')), may hold values from 0 to 3, as said below
- face_slots: int32 [480, 2], P(('grp', 'dom')), may hold values from 0 to 31, as said below
Outputs:
- residual: float32 [480, 80], P(('grp', 'dom'))
- image: float32 [480, 80], P(('grp', 'dom'))
Inputs may be any that keep to these rules, and one draw needn't show every extreme that they name: `side_owner`: an element on the device with grp index g and dom index d has every side owned by a device of grp index g or (g + 1) mod 4; exactly 15 of one device's sides have their owner in each of the two rows. `side_slot`: Take, at grp index g and dom index d, the sides of that device's elements owned in row g together with the sides of the device at grp index (g - 1) mod 4 and the same dom index owned in row g: among those with their owner at one dom index, the slots are distinct. Every element side's receive position is named by exactly one entry of face_slots at its owner, and every entry names one side; each face has two sides of different elements.
All inputs are finite; a program needn't handle non-finite values.
Results may differ from a plain program's by a relative error of at most 0.0065.
Values may be sent and summed in bfloat16 or wider, within the bound.
A program may use at most 64 MiB of HBM per device.

v0:
```python
import functools

import jax
import jax.numpy as jnp
from jax import lax
from jax.experimental import pallas as pl
from jax.experimental.pallas import tpu as pltpu
from jax.sharding import PartitionSpec as P

F32 = jnp.float32
BF16 = jnp.bfloat16
LANES = 128
ROWS = 8
LINK = jnp.bfloat16
MESH = pl.DeviceIdType.MESH


def iota(shape, axis):
    return lax.broadcasted_iota(jnp.int32, shape, axis)


def dot_nn(a, b):
    return jnp.dot(a, b, preferred_element_type=F32)


def dot_nt(a, b):
    return lax.dot_general(a, b, (((1,), (1,)), ((), ())), preferred_element_type=F32)


def kernel(
    grps,
    doms,
    inv_hbm,
    lt_hbm,
    tl_hbm,
    tt_hbm,
    lrhs_hbm,
    trhs_hbm,
    state_hbm,
    owner_hbm,
    slot_hbm,
    face_hbm,
    out_ref,
    lrhs_ref,
    trhs_ref,
    state_ref,
    owner_ref,
    slot_ref,
    face_ref,
    inv_v,
    lt_v,
    tl_v,
    tt_v,
    schur_v,
    state_v,
    down_src,
    down_dst,
    term_src,
    term_dst,
    load_sem,
    small_sem,
    down_send,
    down_recv,
    term_send,
    term_recv,
):
    g = lax.axis_index("grp")
    d = lax.axis_index("dom")
    elements = inv_hbm.shape[0]
    width = tt_hbm.shape[1]
    faces = face_ref.shape[1]
    fd = state_ref.shape[1]
    per_elem = owner_ref.shape[1]
    cap = 2 * ((faces + doms - 1) // doms)
    span = doms * cap
    positions = doms * ROWS
    table = 2 * positions
    face_rows = state_v.shape[0]
    wide = (width // LANES + 1) * LANES
    up_g = lax.rem(g + 1, grps)
    dn_g = lax.rem(g + grps - 1, grps)

    def loads(e):
        pairs = (
            (inv_hbm, inv_v.at[e]),
            (lt_hbm, lt_v.at[e, pl.ds(0, width)]),
            (tl_hbm, tl_v.at[e]),
            (tt_hbm, tt_v.at[e]),
        )
        return [
            pltpu.make_async_copy(src.at[e], dst, load_sem.at[e, i])
            for i, (src, dst) in enumerate(pairs)
        ]

    smalls = [
        pltpu.make_async_copy(src, dst, small_sem.at[i])
        for i, (src, dst) in enumerate(
            (
                (owner_hbm, owner_ref),
                (slot_hbm, slot_ref),
                (face_hbm, face_ref),
                (state_hbm, state_ref),
                (lrhs_hbm, lrhs_ref),
                (trhs_hbm, trhs_ref),
            )
        )
    ]
    for copy in smalls:
        copy.start()

    barrier = pltpu.get_barrier_semaphore()
    for j in range(doms):
        peer = lax.rem(d + j, doms)
        for row in (up_g, dn_g) if j == 0 else (g, up_g, dn_g):
            pl.semaphore_signal(barrier, inc=1, device_id=(row, peer), device_id_type=MESH)

    for e in range(elements):
        for copy in loads(e):
            copy.start()

    for copy in smalls:
        copy.wait()

    def padded(pos):
        return pos // cap * ROWS + lax.rem(pos, cap)

    raw = [[face_ref[i, f] for f in range(faces)] for i in range(2)]
    lane8 = iota((ROWS, LANES), 1)
    row1 = iota((ROWS, 1), 0)
    face_iota = iota((face_rows, 1), 0)
    pos_iota = iota((positions, LANES), 0)
    hits, face_cols = [], []
    for i in range(2):
        row = jnp.full((ROWS, LANES), -1, jnp.int32)
        col = jnp.full((face_rows, 1), -1, jnp.int32)
        for f in range(faces):
            row = jnp.where(lane8 == f, padded(raw[i][f]), row)
            col = jnp.where(face_iota == f, raw[i][f], col)
        hits.append(jnp.where(pos_iota == row[0:1, :], 1.0, 0.0).astype(BF16)[:, :face_rows])
        face_cols.append(col)

    srow = jnp.full((ROWS, LANES), -1, jnp.int32)
    fetch_cols, base_cols, dom_cols, pos_cols = [], [], [], []
    low = jnp.int32(0)
    high = jnp.int32(0)
    for k in range(per_elem):
        fetch_col = jnp.full((ROWS, 1), -1, jnp.int32)
        base_col = jnp.full((ROWS, 1), -4 * doms * span, jnp.int32)
        dom_col = jnp.zeros((ROWS, 1), jnp.int32)
        pos_col = jnp.zeros((ROWS, 1), jnp.int32)
        for e in range(elements):
            owner = owner_ref[e, k]
            own_g = owner // doms
            own_d = owner - own_g * doms
            slot = slot_ref[e, k]
            lift = jnp.where(own_g == g, 0, 1)
            hit = row1 == e
            fetch_col = jnp.where(hit, lift * positions + own_d * ROWS + slot, fetch_col)
            base_col = jnp.where(hit, (2 * lift * doms + own_d) * span + 1, base_col)
            dom_col = jnp.where(hit, own_d, dom_col)
            pos_col = jnp.where(hit, d * cap + slot + 1, pos_col)
            place = jnp.where(own_g == g, low, face_rows + high)
            srow = jnp.where(lane8 == k * ROWS + e, place, srow)
            high = high + lift
            low = low + 1 - lift
        fetch_cols.append(fetch_col)
        base_cols.append(base_col)
        dom_cols.append(dom_col)
        pos_cols.append(pos_col)
    side_rows = per_elem * ROWS
    fetch_hot = jnp.where(
        iota((side_rows, table), 1) == jnp.concatenate(fetch_cols, axis=0), 1.0, 0.0
    ).astype(BF16)
    place_hot = jnp.where(iota((2 * face_rows, LANES), 0) == srow[0:1, :], 1.0, 0.0).astype(BF16)[
        :, :side_rows
    ]
    base = jnp.concatenate(base_cols, axis=0).astype(F32)
    lane_s = iota((side_rows, LANES), 1)
    stamp = jnp.where(
        lane_s == fd,
        jnp.concatenate(dom_cols, axis=0).astype(F32),
        jnp.where(lane_s == fd + 1, jnp.concatenate(pos_cols, axis=0).astype(F32), 0.0),
    ).astype(BF16)

    state_v[...] = jnp.zeros_like(state_v)
    state_v[0:faces, 0:fd] = state_ref[...].astype(F32)
    spare = wide - width
    rhs = lrhs_ref[...].astype(F32)
    spare_row = iota((spare, rhs.shape[1]), 0)
    for e in range(elements):
        lt_v[e, width:wide, :] = jnp.where(spare_row == 0, rhs[e : e + 1, :], 0.0).astype(BF16)

    def down_copies(incoming=False):
        copies = []
        for j in range(doms):
            peer = lax.rem(d + j, doms)
            for lift, row in ((0, g), (1, dn_g)):
                if j == 0 and lift == 0:
                    continue
                copies.append(
                    pltpu.make_async_remote_copy(
                        src_ref=down_src.at[peer],
                        dst_ref=down_dst.at[lift, peer if incoming else d],
                        send_sem=down_send.at[lift, peer],
                        recv_sem=down_recv.at[lift, peer if incoming else d],
                        device_id=(row, peer),
                        device_id_type=MESH,
                    )
                )
        return copies

    regions = ((0, g), (1, up_g), (0, dn_g), (1, g))

    def term_copies(turn, incoming=False):
        copies = []
        for j in range(doms):
            peer = lax.rem(d + j, doms)
            for r in range(4 - 2 * turn):
                half, row = regions[r]
                if j == 0 and r in (0, 3):
                    continue
                copies.append(
                    pltpu.make_async_remote_copy(
                        src_ref=term_src.at[turn, half],
                        dst_ref=term_dst.at[turn, r, peer if incoming else d],
                        send_sem=term_send.at[turn, r, peer],
                        recv_sem=term_recv.at[turn, r, peer if incoming else d],
                        device_id=(row, peer),
                        device_id_type=MESH,
                    )
                )
        return copies

    def send_state():
        lane_f = iota((face_rows, LANES), 1)
        rows = dot_nn(hits[0] + hits[1], state_v[...].astype(BF16))
        for i in range(2):
            other = jnp.where(lane_f == fd, face_cols[1 - i].astype(F32), 0.0).astype(BF16)
            rows = rows + dot_nn(hits[i], other)
        down_src[...] = rows.reshape(doms, ROWS, LANES).astype(LINK)
        for copy in down_copies():
            copy.start()
        down_dst[0, d] = down_src[d]

    def spread_faces(sides):
        total = jnp.zeros((ROWS, wide), F32)
        for k in range(per_elem):
            piece = jnp.concatenate(
                [sides[k * ROWS : (k + 1) * ROWS, :], jnp.zeros((ROWS, wide - LANES), F32)], axis=1
            )
            total = total + (piece if k == 0 else pltpu.roll(piece, k * fd, 1))
        return total

    row_wide = iota((ROWS, width), 0)

    def apply(vector):
        total = jnp.zeros((ROWS, width), F32)
        for e in range(elements):
            total = total + jnp.where(row_wide == e, dot_nt(vector.astype(BF16), schur_v[e]), 0.0)
        return total

    lane_fd = iota((ROWS, LANES), 1) < fd

    def send_terms(turn, terms):
        full = jnp.concatenate([terms, jnp.zeros((ROWS, wide - width), F32)], axis=1)
        pieces = []
        for k in range(per_elem):
            moved = full if k == 0 else pltpu.roll(full, wide - k * fd, 1)
            pieces.append(jnp.where(lane_fd, moved[:, :LANES], 0.0))
        sides = jnp.concatenate(pieces, axis=0).astype(BF16)
        rows = dot_nn(place_hot, sides + stamp)
        term_src[turn] = rows.reshape(2, face_rows, LANES).astype(BF16)
        for copy in term_copies(turn):
            copy.start()
        term_dst[turn, 0, d] = term_src[turn, 0]
        if turn == 0:
            term_dst[turn, 3, d] = term_src[turn, 1]
        return sides.astype(F32)

    def element(e, carry):
        @pl.when(e == elements // 2)
        def _():
            pl.semaphore_wait(barrier, 3 * doms - 1)
            send_state()

        for copy in loads(e):
            copy.wait()
        coupled = dot_nt(inv_v[e], lt_v[e]).astype(BF16)
        removed = dot_nn(tl_v[e], coupled)
        edge = width // LANES * LANES
        schur_v[e, :, edge:wide] = (-removed[:, edge:wide]).astype(BF16)
        schur_v[e, :, 0:width] = (tt_v[e].astype(F32) - removed[:, 0:width]).astype(BF16)
        return carry

    lax.fori_loop(0, elements, element, 0)

    for copy in down_copies(True):
        copy.wait_recv()
    got = down_dst[...].astype(F32).reshape(table, LANES).astype(BF16)
    sides = dot_nn(fetch_hot, got)
    lane_side = iota((side_rows, LANES), 1)
    target = base + sides[:, fd : fd + 1]
    faces_in = spread_faces(jnp.where(lane_side < fd, sides, 0.0))
    vector = jnp.where(iota((ROWS, wide), 1) == width, -1.0, faces_in)
    trhs = jnp.concatenate(
        [trhs_ref[...].astype(F32), jnp.zeros((ROWS - elements, width), F32)], axis=0
    )
    mine = send_terms(0, apply(vector) - trhs)

    rows_own = 2 * doms * face_rows
    rows_all = 2 * rows_own
    for copy in term_copies(0, True):
        copy.wait_recv()
    first = term_dst[0].reshape(rows_all, LANES)
    lane_k = iota((ROWS, LANES), 1)
    weights = jnp.where(lane_k == fd, float(span), jnp.where(lane_k == fd + 1, 1.0, 0.0))
    keys = dot_nt(weights.astype(BF16), first)[0:1, :]
    keys = keys + jnp.where(iota((1, rows_all), 1) >= rows_own, 2.0 * doms * span, 0.0)
    partner = dot_nn(jnp.where(keys == target, 1.0, 0.0).astype(BF16), first)
    total = jnp.where(lane_side < fd, mine + partner, 0.0)
    send_terms(1, apply(spread_faces(total)))

    own_keys = keys[:, :rows_own]
    ask = [jnp.where(col < 0, -1, d * span + 1 + col).astype(F32) for col in face_cols]
    pick = (
        jnp.where(own_keys == ask[0], 1.0, 0.0) + jnp.where(own_keys == ask[1], 1.0, 0.0)
    ).astype(BF16)
    out_ref[0] = dot_nn(pick, first[:rows_own])
    for copy in down_copies() + term_copies(0):
        copy.wait_send()
    for copy in term_copies(1, True):
        copy.wait_recv()
    out_ref[1] = dot_nn(pick, term_dst[1, 0:2].reshape(rows_own, LANES))
    for copy in term_copies(1):
        copy.wait_send()


def on_device(grps, doms, *args):
    inv, lt, tl, tt, lrhs, trhs, state, owner, slot, faces = args
    elements, interior = inv.shape[0], inv.shape[1]
    width = tt.shape[1]
    wide = (width // LANES + 1) * LANES
    lt = jnp.swapaxes(lt, 1, 2)
    n_faces, fd = state.shape
    face_rows = (n_faces + 15) // 16 * 16
    vmem = pl.BlockSpec(memory_space=pltpu.VMEM)
    anys = pl.BlockSpec(memory_space=pl.ANY)
    out = pl.pallas_call(
        functools.partial(kernel, grps, doms),
        out_shape=jax.ShapeDtypeStruct((2, face_rows, LANES), F32),
        in_specs=[anys] * 10,
        out_specs=vmem,
        scratch_shapes=[
            pltpu.VMEM(lrhs.shape, BF16),
            pltpu.VMEM(trhs.shape, BF16),
            pltpu.VMEM(state.shape, BF16),
            pltpu.SMEM(owner.shape, jnp.int32),
            pltpu.SMEM(slot.shape, jnp.int32),
            pltpu.SMEM((2, n_faces), jnp.int32),
            pltpu.VMEM(inv.shape, BF16),
            pltpu.VMEM((elements, wide, interior), BF16),
            pltpu.VMEM(tl.shape, BF16),
            pltpu.VMEM(tt.shape, BF16),
            pltpu.VMEM((elements, width, wide), BF16),
            pltpu.VMEM((face_rows, LANES), F32),
            pltpu.VMEM((doms, ROWS, LANES), LINK),
            pltpu.VMEM((2, doms, ROWS, LANES), LINK),
            pltpu.VMEM((2, 2, face_rows, LANES), BF16),
            pltpu.VMEM((2, 4, doms, face_rows, LANES), BF16),
            pltpu.SemaphoreType.DMA((elements, 4)),
            pltpu.SemaphoreType.DMA((6,)),
            pltpu.SemaphoreType.DMA((2, doms)),
            pltpu.SemaphoreType.DMA((2, doms)),
            pltpu.SemaphoreType.DMA((2, 4, doms)),
            pltpu.SemaphoreType.DMA((2, 4, doms)),
        ],
        compiler_params=pltpu.CompilerParams(
            collective_id=0, has_side_effects=True, vmem_limit_bytes=60 * 1024 * 1024
        ),
    )(inv, lt, tl, tt, lrhs, trhs, state, owner, slot, faces.T)
    return out[0, :n_faces, :fd], out[1, :n_faces, :fd]


def solution(mesh):
    lead = ("grp", "dom")
    specs = (P(lead, None, None),) * 4 + (P(lead, None),) * 6
    return jax.shard_map(
        functools.partial(on_device, mesh.shape["grp"], mesh.shape["dom"]),
        mesh=mesh,
        in_specs=specs,
        out_specs=(P(lead, None), P(lead, None)),
        check_vma=False,
    )
```

profile of v0, /device:TPU:0, one launch (start us, length us, event | category | flops | bytes accessed | tf_op | source)
XLA Modules:
  0.0 27.3 jit_solution(18146045149720230723)
XLA Ops:
  0.6 25.3 %shard_map.113 = f32[2,16,128]{2,1,0:T(8,128)} custom-call(bf16[5,640,640]{2,1,0:T(8,128)(2,1)} %inv_hbm.1, bf16[5,480,640]{2,1,0:T(8,128)(2,1)} %bitcast.6, bf16[5,480,640]{2,1,0:T(8,128)(2,1)} %tl_hbm.1, bf16[5,480,480]{2,1,0:T(8,128)(2,1)} %tt_hbm.1, bf16[5,640]{1,0:T(8,128)(2,1)} %lrhs_hbm.1, bf16[5,480]{1,0:T(8,128)(2,1)} %trhs_hbm.1, ...), custom_call_target="tpu_custom_call" | custom-call | tf_op jit(solution)/shard_map/pallas_call | solution.py:348
  25.9 1.3 %slice_bitcast_fusion = (f32[15,80]{1,0:T(8,128)}, f32[15,80]{1,0:T(8,128)}) fusion(f32[2,16,128]{2,1,0:T(8,128)} %shard_map.113), kind=kLoop, calls=%fused_computation | loop fusion | bytes 19200 | tf_op jit(solution)/shard_map/squeeze | solution.py:381
where the time goes:
time: 27.5 us; the launch traced here: 27.3 us
  Pallas kernels  25.3 us (92%)
  local copies, waits for them, and re-layouts  1.32 us (5%)
  between operations  0.64 us (2%)
    pallas_call x1, Pallas kernels, on_device(): pl.pallas_call(functools.partial(kernel, grps, doms), out_shape=jax.Shape...  25.3 us
    squeeze x1, local copies, waits for them, and re-layouts, on_device(): return (out[0, :n_faces, :fd], out[1, :n_faces, :fd])  1.32 us

commit v1 on v0

--- a/solution.py
+++ b/solution.py
@@ -278,7 +278,7 @@
         return sides.astype(F32)
 
     def element(e, carry):
-        @pl.when(e == elements // 2)
+        @pl.when(e == jnp.where(g == 0, 3, 1))
         def _():
             pl.semaphore_wait(barrier, 3 * doms - 1)
             send_state()
@@ -375,9 +375,9 @@
             pltpu.SemaphoreType.DMA((2, 4, doms)),
         ],
         compiler_params=pltpu.CompilerParams(
-            collective_id=0, has_side_effects=True, vmem_limit_bytes=60 * 1024 * 1024
+            collective_id=0, has_side_effects=True, vmem_limit_bytes=24 * 1024 * 1024
         ),
-    )(inv, lt, tl, tt, lrhs, trhs, state, owner, slot, faces.T)
+    )(*[pltpu.with_memory_space_constraint(v, pltpu.HBM) for v in (inv, lt, tl, tt, lrhs, trhs, state, owner, slot, faces.T)])
     return out[0, :n_faces, :fd], out[1, :n_faces, :fd]
 
 

time: 27.5 us -> 26 us (0.945)
  local copies, waits for them, and re-layouts: 1.32 us -> 0.61 us
  Pallas kernels: 25.3 us -> 24.6 us
    pallas_call x1, Pallas kernels: 25.3 us -> 24.6 us  [on_device(): pl.pallas_call(functools.partial(kernel, grps, doms), out_shape=jax.Shape...]
    squeeze x1, local copies, waits for them, and re-layouts: 1.32 us -> 0.61 us  [on_device(): return (out[0, :n_faces, :fd], out[1, :n_faces, :fd])]
where the time goes in v1:
time: 26 us; the launch traced here: 25.8 us
  Pallas kernels  24.6 us (95%)
  between operations  0.64 us (2%)
  local copies, waits for them, and re-layouts  0.61 us (2%)
    pallas_call x1, Pallas kernels, on_device(): pl.pallas_call(functools.partial(kernel, grps, doms), out_shape=jax.Shape...  24.6 us
    squeeze x1, local copies, waits for them, and re-layouts, on_device(): return (out[0, :n_faces, :fd], out[1, :n_faces, :fd])  0.61 us

profile of v1, /device:TPU:0, one launch (start us, length us, event | category | flops | bytes accessed | tf_op | source)
XLA Modules:
  0.0 25.8 jit_solution(11976509923834566373)
XLA Ops:
  0.6 24.6 %shard_map.113 = f32[2,16,128]{2,1,0:T(8,128)S(1)} custom-call(bf16[5,640,640]{2,1,0:T(8,128)(2,1)} %inv_hbm.1, bf16[5,480,640]{2,1,0:T(8,128)(2,1)} %bitcast.6, bf16[5,480,640]{2,1,0:T(8,128)(2,1)} %tl_hbm.1, bf16[5,480,480]{2,1,0:T(8,128)(2,1)} %tt_hbm.1, bf16[5,640]{1,0:T(8,128)(2,1)} %lrhs_hbm.1, bf16[5,480]{1,0:T(8,128)(2,1)} %trhs_hbm.1, ...), custom_call_target="tpu_custom_call" | custom-call | tf_op jit(solution)/shard_map/pallas_call | solution.py:348
  25.2 0.6 %slice_bitcast_fusion = (f32[15,80]{1,0:T(8,128)}, f32[15,80]{1,0:T(8,128)}) fusion(f32[2,16,128]{2,1,0:T(8,128)S(1)} %shard_map.113), kind=kLoop, calls=%fused_computation | loop fusion | bytes 19200 | tf_op jit(solution)/shard_map/squeeze | solution.py:381

commit v2 on v1

--- a/solution.py
+++ b/solution.py
@@ -278,7 +278,7 @@
         return sides.astype(F32)
 
     def element(e, carry):
-        @pl.when(e == jnp.where(g == 0, 3, 1))
+        @pl.when(e == jnp.where(g == 0, jnp.where(d < 2, 3, 2), 1))
         def _():
             pl.semaphore_wait(barrier, 3 * doms - 1)
             send_state()

time: 26 us -> 25.2 us (0.969)
  Pallas kernels: 24.6 us -> 23.7 us
    pallas_call x1, Pallas kernels: 24.6 us -> 23.7 us  [on_device(): pl.pallas_call(functools.partial(kernel, grps, doms), out_shape=jax.Shape...]
where the time goes in v2:
time: 25.2 us; the launch traced here: 25 us
  Pallas kernels  23.7 us (94%)
  between operations  0.64 us (3%)
  local copies, waits for them, and re-layouts  0.61 us (2%)
    pallas_call x1, Pallas kernels, on_device(): pl.pallas_call(functools.partial(kernel, grps, doms), out_shape=jax.Shape...  23.7 us
    squeeze x1, local copies, waits for them, and re-layouts, on_device(): return (out[0, :n_faces, :fd], out[1, :n_faces, :fd])  0.61 us

profile of v2, /device:TPU:0, one launch (start us, length us, event | category | flops | bytes accessed | tf_op | source)
XLA Modules:
  0.0 25.0 jit_solution(9223385397601839217)
XLA Ops:
  0.6 23.7 %shard_map.113 = f32[2,16,128]{2,1,0:T(8,128)S(1)} custom-call(bf16[5,640,640]{2,1,0:T(8,128)(2,1)} %inv_hbm.1, bf16[5,480,640]{2,1,0:T(8,128)(2,1)} %bitcast.6, bf16[5,480,640]{2,1,0:T(8,128)(2,1)} %tl_hbm.1, bf16[5,480,480]{2,1,0:T(8,128)(2,1)} %tt_hbm.1, bf16[5,640]{1,0:T(8,128)(2,1)} %lrhs_hbm.1, bf16[5,480]{1,0:T(8,128)(2,1)} %trhs_hbm.1, ...), custom_call_target="tpu_custom_call" | custom-call | tf_op jit(solution)/shard_map/pallas_call | solution.py:348
  24.4 0.6 %slice_bitcast_fusion = (f32[15,80]{1,0:T(8,128)}, f32[15,80]{1,0:T(8,128)}) fusion(f32[2,16,128]{2,1,0:T(8,128)S(1)} %shard_map.113), kind=kLoop, calls=%fused_computation | loop fusion | bytes 19200 | tf_op jit(solution)/shard_map/squeeze | solution.py:381

commit v3 on v2

--- a/solution.py
+++ b/solution.py
@@ -109,9 +109,9 @@
         copy.start()
 
     barrier = pltpu.get_barrier_semaphore()
-    for j in range(doms):
-        peer = lax.rem(d + j, doms)
-        for row in (up_g, dn_g) if j == 0 else (g, up_g, dn_g):
+    for row in (up_g, dn_g, g):
+        for j in range(1 if row is g else 0, doms):
+            peer = lax.rem(d + j, doms)
             pl.semaphore_signal(barrier, inc=1, device_id=(row, peer), device_id_type=MESH)
 
     for e in range(elements):
@@ -202,7 +202,7 @@
                         src_ref=down_src.at[peer],
                         dst_ref=down_dst.at[lift, peer if incoming else d],
                         send_sem=down_send.at[lift, peer],
-                        recv_sem=down_recv.at[lift, peer if incoming else d],
+                        recv_sem=down_recv.at[0],
                         device_id=(row, peer),
                         device_id_type=MESH,
                     )
@@ -224,7 +224,7 @@
                         src_ref=term_src.at[turn, half],
                         dst_ref=term_dst.at[turn, r, peer if incoming else d],
                         send_sem=term_send.at[turn, r, peer],
-                        recv_sem=term_recv.at[turn, r, peer if incoming else d],
+                        recv_sem=term_recv.at[turn],
                         device_id=(row, peer),
                         device_id_type=MESH,
                     )
@@ -240,7 +240,7 @@
         down_src[...] = rows.reshape(doms, ROWS, LANES).astype(LINK)
         for copy in down_copies():
             copy.start()
-        down_dst[0, d] = down_src[d]
+        pltpu.make_async_copy(down_src.at[d], down_dst.at[0, d], down_recv.at[0]).start()
 
     def spread_faces(sides):
         total = jnp.zeros((ROWS, wide), F32)
@@ -272,9 +272,10 @@
         term_src[turn] = rows.reshape(2, face_rows, LANES).astype(BF16)
         for copy in term_copies(turn):
             copy.start()
-        term_dst[turn, 0, d] = term_src[turn, 0]
-        if turn == 0:
-            term_dst[turn, 3, d] = term_src[turn, 1]
+        for r in (0, 3) if turn == 0 else (0,):
+            pltpu.make_async_copy(
+                term_src.at[turn, regions[r][0]], term_dst.at[turn, r, d], term_recv.at[turn]
+            ).start()
         return sides.astype(F32)
 
     def element(e, carry):
@@ -294,8 +295,7 @@
 
     lax.fori_loop(0, elements, element, 0)
 
-    for copy in down_copies(True):
-        copy.wait_recv()
+    pltpu.make_async_copy(down_dst, down_dst, down_recv.at[0]).wait()
     got = down_dst[...].astype(F32).reshape(table, LANES).astype(BF16)
     sides = dot_nn(fetch_hot, got)
     lane_side = iota((side_rows, LANES), 1)
@@ -309,8 +309,7 @@
 
     rows_own = 2 * doms * face_rows
     rows_all = 2 * rows_own
-    for copy in term_copies(0, True):
-        copy.wait_recv()
+    pltpu.make_async_copy(term_dst.at[0], term_dst.at[0], term_recv.at[0]).wait()
     first = term_dst[0].reshape(rows_all, LANES)
     lane_k = iota((ROWS, LANES), 1)
     weights = jnp.where(lane_k == fd, float(span), jnp.where(lane_k == fd + 1, 1.0, 0.0))
@@ -326,13 +325,10 @@
         jnp.where(own_keys == ask[0], 1.0, 0.0) + jnp.where(own_keys == ask[1], 1.0, 0.0)
     ).astype(BF16)
     out_ref[0] = dot_nn(pick, first[:rows_own])
-    for copy in down_copies() + term_copies(0):
+    for copy in down_copies() + term_copies(0) + term_copies(1):
         copy.wait_send()
-    for copy in term_copies(1, True):
-        copy.wait_recv()
+    pltpu.make_async_copy(term_dst.at[1, 0:2], term_dst.at[1, 0:2], term_recv.at[1]).wait()
     out_ref[1] = dot_nn(pick, term_dst[1, 0:2].reshape(rows_own, LANES))
-    for copy in term_copies(1):
-        copy.wait_send()
 
 
 def on_device(grps, doms, *args):
@@ -370,9 +366,9 @@
             pltpu.SemaphoreType.DMA((elements, 4)),
             pltpu.SemaphoreType.DMA((6,)),
             pltpu.SemaphoreType.DMA((2, doms)),
-            pltpu.SemaphoreType.DMA((2, doms)),
+            pltpu.SemaphoreType.DMA((1,)),
             pltpu.SemaphoreType.DMA((2, 4, doms)),
-            pltpu.SemaphoreType.DMA((2, 4, doms)),
+            pltpu.SemaphoreType.DMA((2,)),
         ],
         compiler_params=pltpu.CompilerParams(
             collective_id=0, has_side_effects=True, vmem_limit_bytes=24 * 1024 * 1024

time: 25.2 us -> 24.3 us (0.964)
  Pallas kernels: 23.7 us -> 22.9 us
    pallas_call x1, Pallas kernels: 23.7 us -> 22.9 us  [on_device(): pl.pallas_call(functools.partial(kernel, grps, doms), out_shape=jax.Shape...]
where the time goes in v3:
time: 24.3 us; the launch traced here: 24.1 us
  Pallas kernels  22.9 us (94%)
  between operations  0.64 us (3%)
  local copies, waits for them, and re-layouts  0.61 us (3%)
    pallas_call x1, Pallas kernels, on_device(): pl.pallas_call(functools.partial(kernel, grps, doms), out_shape=jax.Shape...  22.9 us
    squeeze x1, local copies, waits for them, and re-layouts, on_device(): return (out[0, :n_faces, :fd], out[1, :n_faces, :fd])  0.61 us

profile of v3, /device:TPU:0, one launch (start us, length us, event | category | flops | bytes accessed | tf_op | source)
XLA Modules:
  0.0 24.1 jit_solution(7382595448802947747)
XLA Ops:
  0.6 22.9 %shard_map.113 = f32[2,16,128]{2,1,0:T(8,128)S(1)} custom-call(bf16[5,640,640]{2,1,0:T(8,128)(2,1)} %inv_hbm.1, bf16[5,480,640]{2,1,0:T(8,128)(2,1)} %bitcast.6, bf16[5,480,640]{2,1,0:T(8,128)(2,1)} %tl_hbm.1, bf16[5,480,480]{2,1,0:T(8,128)(2,1)} %tt_hbm.1, bf16[5,640]{1,0:T(8,128)(2,1)} %lrhs_hbm.1, bf16[5,480]{1,0:T(8,128)(2,1)} %trhs_hbm.1, ...), custom_call_target="tpu_custom_call" | custom-call | tf_op jit(solution)/shard_map/pallas_call | solution.py:344
  23.5 0.6 %slice_bitcast_fusion = (f32[15,80]{1,0:T(8,128)}, f32[15,80]{1,0:T(8,128)}) fusion(f32[2,16,128]{2,1,0:T(8,128)S(1)} %shard_map.113), kind=kLoop, calls=%fused_computation | loop fusion | bytes 19200 | tf_op jit(solution)/shard_map/squeeze | solution.py:377
